TPU v7x, 512 devices: a whole 4x8x8 slice. The times are simulated.
512 devices in a mesh: ctx: 64 (over y_hi, x, z), exp: 8 (over y_lo, core).
Axes of the slice: x: 4, y: 8 (y_hi: 2, y_lo: 4; y = y_hi * 4 + y_lo), z: 8, core: 2. Of those that a mesh axis runs over, the one named last changes fastest.
Arguments:
- queries: bfloat16 [4096, 6144], P('ctx', 'exp'), may hold values from -5 to 5
- keys: bfloat16 [4096, 1024], P('ctx', 'exp'), may hold values from -5 to 5
- values: bfloat16 [4096, 1024], P('ctx', 'exp'), may hold values from -16 to 16
- residual: bfloat16 [4096, 6144], P('ctx', 'exp'), may hold values from -25 to 25
- norm_gain: float32 [6144], P('exp'), may hold values from 0.5 to 1.5
- routes: int32 [4096, 1], P('ctx'), may hold values from 0 to 3; in each aligned block of 64 rows (0 to 63, 64 to 127, ...) at most 24 rows name the same one
- route_weight: float32 [4096], P('ctx'), may hold values from 0.25 to 1
- w_gate: bfloat16 [65536, 6144], P('ctx', 'exp'), may hold values from -0.078125 to 0.078125
- w_up: bfloat16 [65536, 6144], P('ctx', 'exp'), may hold values from -0.078125 to 0.078125
- w_down: bfloat16 [65536, 6144], P('ctx', 'exp'), may hold values from -0.046875 to 0.046875
Outputs:
- moe_out: bfloat16 [4096, 6144], P('ctx', 'exp')
Inputs may be any that keep to these rules, and one draw needn't show every extreme that they name: `routes`: within the 64 rows of one device, at most 24 tokens have the same route.
All inputs are finite; a program needn't handle non-finite values.
Results may differ from a plain program's by a relative error of at most 0.029.
Values may be sent and summed in bfloat16 or wider, within the bound.
No kernel may reach another device: no remote copies, remote signals or barrier semaphores. Data moves between devices by JAX's collectives and lax.ppermute only.
A program may use at most 64 MiB of HBM per device.

v0:
```python
import math
import jax
import jax.numpy as jnp
from jax import lax
from jax.sharding import PartitionSpec as P

D = 6144
HD = 128
EXPERTS = 4
CAP = 24


def body(queries, keys, values, residual, norm_gain, routes, route_weight, w_gate, w_up, w_down):
    tok_rows = queries.shape[0]
    heads_kv = keys.shape[1] // HD
    heads_query = queries.shape[1] // HD
    group_size = heads_query // heads_kv
    first_pos = lax.axis_index("ctx") * tok_rows
    last_pos = first_pos + tok_rows - 1
    score_scale = 1.0 / math.sqrt(HD)
    query_block = (
        queries.reshape(tok_rows, heads_kv, group_size, HD)
        .transpose(1, 2, 0, 3)
        .reshape(heads_kv, group_size * tok_rows, HD)
    )
    query_pos = first_pos + jnp.tile(jnp.arange(tok_rows, dtype=jnp.int32), group_size)
    initial = (
        jnp.full((heads_kv, group_size * tok_rows), -1e30, jnp.float32),
        jnp.zeros((heads_kv, group_size * tok_rows), jnp.float32),
        jnp.zeros((heads_kv, group_size * tok_rows, HD), jnp.float32),
    )
    key_shard = lax.all_gather(keys, "ctx", axis=0, tiled=True)
    value_shard = lax.all_gather(values, "ctx", axis=0, tiled=True)
    key_count = key_shard.shape[0]

    def compute(status):
        running_max, running_sum, running_acc = status
        key_block = key_shard.reshape(key_count, heads_kv, HD).transpose(1, 0, 2)
        value_block = value_shard.reshape(key_count, heads_kv, HD).transpose(1, 0, 2)
        scores = (
            jnp.einsum("gqd,gkd->gqk", query_block, key_block, preferred_element_type=jnp.float32)
            * score_scale
        )
        key_pos = jnp.arange(key_count, dtype=jnp.int32)
        allowed = (key_pos[None, :] <= query_pos[:, None])[None, :, :]
        masked = jnp.where(allowed, scores, -1e30)
        fresh_max = jnp.maximum(running_max, jnp.max(masked, axis=2))
        weights = jnp.where(allowed, jnp.exp(masked - fresh_max[:, :, None]), 0.0)
        new_sum = jnp.sum(weights, axis=2)
        products = jnp.einsum(
            "gqk,gkd->gqd",
            weights.astype(jnp.bfloat16),
            value_block,
            preferred_element_type=jnp.float32,
        )
        return (fresh_max, new_sum, products)

    def unchanged(status):
        return status

    final_max, final_sum, final_acc = lax.cond(
        jnp.int32(0) <= last_pos, compute, unchanged, initial
    )
    attn_heads = final_acc / final_sum[:, :, None]
    attn = (
        attn_heads.reshape(heads_kv, group_size, tok_rows, HD)
        .transpose(2, 0, 1, 3)
        .reshape(tok_rows, heads_query * HD)
        .astype(jnp.bfloat16)
    )
    mixed = residual.astype(jnp.float32) + attn.astype(jnp.float32)
    local_squares = jnp.sum(mixed * mixed, axis=1)
    total_squares = lax.psum(local_squares, "exp")
    normed = (mixed * lax.rsqrt(total_squares / D + 1e-05)[:, None] * norm_gain[None, :]).astype(
        jnp.bfloat16
    )
    feat_local = normed.shape[1]
    chosen = routes[:, 0]
    expert_ids = jnp.arange(EXPERTS, dtype=jnp.int32)
    onehot = (chosen[:, None] == expert_ids[None, :]).astype(jnp.int32)
    slot_index = jnp.sum((jnp.cumsum(onehot, axis=0) - 1) * onehot, axis=1)
    slot_ids = jnp.arange(CAP, dtype=jnp.int32)
    select = (
        (chosen[None, None, :] == expert_ids[:, None, None])
        & (slot_index[None, None, :] == slot_ids[None, :, None])
    ).astype(jnp.float32)
    packed = jnp.einsum(
        "ect,td->ecd", select.astype(jnp.bfloat16), normed, preferred_element_type=jnp.float32
    ).astype(jnp.bfloat16)
    ctx_count = lax.axis_size("ctx")
    members = ctx_count // EXPERTS
    outgoing = jnp.broadcast_to(packed[:, None], (EXPERTS, members, CAP, feat_local)).reshape(
        ctx_count, CAP, feat_local
    )
    incoming = lax.all_to_all(outgoing, "ctx", split_axis=0, concat_axis=0, tiled=True)
    slot_count = incoming.shape[1]
    flat_rows = incoming.reshape(ctx_count * slot_count, feat_local)
    gate_part = jnp.einsum("rd,fd->rf", flat_rows, w_gate, preferred_element_type=jnp.float32)
    up_part = jnp.einsum("rd,fd->rf", flat_rows, w_up, preferred_element_type=jnp.float32)
    gate_full = lax.psum(gate_part.astype(jnp.bfloat16), "exp").astype(jnp.float32)
    up_full = lax.psum(up_part.astype(jnp.bfloat16), "exp").astype(jnp.float32)
    hidden = (jax.nn.silu(gate_full) * up_full).astype(jnp.bfloat16)
    down_part = jnp.dot(hidden, w_down, preferred_element_type=jnp.float32).reshape(
        ctx_count, slot_count, feat_local
    )
    returned = lax.all_to_all(
        down_part.astype(jnp.bfloat16), "ctx", split_axis=0, concat_axis=0, tiled=True
    ).astype(down_part.dtype)
    combined = returned.reshape(EXPERTS, members, CAP, feat_local).sum(axis=1)
    moe_rows = jnp.einsum(
        "ect,ecd->td",
        select,
        combined,
        precision=lax.Precision.HIGHEST,
        preferred_element_type=jnp.float32,
    )
    return (route_weight[:, None] * moe_rows).astype(jnp.bfloat16)


def solution(mesh):
    in_specs = (
        P("ctx", "exp"),
        P("ctx", "exp"),
        P("ctx", "exp"),
        P("ctx", "exp"),
        P("exp"),
        P("ctx", None),
        P("ctx"),
        P("ctx", "exp"),
        P("ctx", "exp"),
        P("ctx", "exp"),
    )
    out_specs = P("ctx", "exp")
    return jax.shard_map(body, mesh=mesh, in_specs=in_specs, out_specs=out_specs, check_vma=False)
```

profile of v0, /device:TPU:40, one launch (start us, length us, event | category | flops | bytes accessed | tf_op | source)
XLA Modules:
  0.0 611.7 jit_solution(5762565364103222619)
XLA Ops:
  6.5 0.0 copy-start
  6.5 0.0 all-gather.3.cloned.1.call-start
  6.5 0.7 all-gather.3.cloned.1.call-update
  7.3 0.0 all-gather.5.cloned.1.call-start
  7.3 0.7 all-gather.5.cloned.1.call-update
  8.0 0.0 all-reduce.3.cloned.1.call-start
  8.1 0.7 fusion.22
  8.8 0.1 reduce_window_sum.11
  8.9 1.0 reshape.116
  9.9 0.8 select_reduce_fusion
  10.8 0.7 iota_compare_fusion.3
  11.4 128.2 %all-gather.3.cloned.1.call-done = bf16[4096,128]{1,0:T(8,128)(2,1)} async-done(((bf16[64,128]{1,0:T(8,128)(2,1)}), bf16[4096,128]{1,0:T(8,128)(2,1)}) %all-gather.3.cloned.1.call-update) | async-done | bytes 1048592 | tf_op jit(solution)/shard_map/all_gather | solution.py:32
  139.6 125.6 %all-gather.5.cloned.1.call-done = bf16[4096,128]{1,0:T(8,128)(2,1)} async-done(((bf16[64,128]{1,0:T(8,128)(2,1)}), bf16[4096,128]{1,0:T(8,128)(2,1)}) %all-gather.5.cloned.1.call-update) | async-done | bytes 1048592 | tf_op jit(solution)/shard_map/all_gather | solution.py:33
  265.2 0.0 copy-start.1
  265.2 0.0 copy-start.2
  265.2 6.3 %conditional.1 = (f32[1,384]{1,0:T(1,128)S(1)}, f32[1,384,128]{2,1,0:T(8,128)S(1)}) conditional(s32[]{:T(128)} %convert_element_type.72, () %tuple.13, (s32[]{:T(128)}, s32[6,64]{1,0:T(8,128)S(1)}, bf16[1,6,64,128]{3,1,2,0:T(8,128)(2,1)S(1)}, bf16[4096,128]{1,0:T(8,128)(2,1)}, bf16[4096,128]{1,0:T(8,128)(2,1)}) %tuple.26), branch_computations={%region_2.0_spmd, %region_3.6_spmd} | conditional | flops 824180736 | bytes 25680432 | solution.py:61
  265.2 0.1 add.30
  265.3 0.0 copy-start.6
  265.3 2.6 fusion.29
  268.0 0.0 copy-done.6
  268.0 1.9 fusion.4
  269.9 1.6 fusion.1
  271.5 0.1 divide_convert_fusion
  271.7 0.1 copy.13
  271.7 0.0 copy-done.1
  271.7 0.1 multiply_reduce_fusion
  271.9 10.3 %psum.21 = f32[64]{0:T(128)S(1)} all-reduce(f32[64]{0:T(128)S(1)} %multiply_reduce_fusion), channel_id=1, replica_groups=mesh['ctx'=64,'exp'=8] {'exp'}, use_global_device_ids=true, to_apply=%region_7.8 | all-reduce | flops 64 | bytes 512 | tf_op jit(solution)/shard_map/psum | solution.py:73
  282.2 0.0 copy-done.2
  282.2 0.2 convolution_convert_fusion.3
  282.4 0.2 broadcast_in_dim.22
  282.6 69.9 %all_to_all.10 = bf16[64,24,768]{2,1,0:T(8,128)(2,1)S(1)} all-to-all(bf16[64,24,768]{2,1,0:T(8,128)(2,1)S(1)} %bitcast.42), channel_id=1, replica_groups=mesh['ctx'=64,'exp'=8] {'ctx'}, dimensions={0} | all-to-all | bytes 4718592 | tf_op jit(solution)/shard_map/all_to_all | solution.py:95
  352.5 0.0 copy-done
  352.5 0.0 copy-start.4
  352.5 4.2 convolution_convert_fusion
  356.7 0.0 copy-done.4
  356.7 4.2 convolution_convert_fusion.1
  360.8 0.0 copy-start.5
  360.8 0.0 all-reduce.3.cloned.1.call-update
  360.9 154.0 %all-reduce.3.cloned.1.call-done = (bf16[1536,1024]{1,0:T(8,128)(2,1)}, bf16[1536,1024]{1,0:T(8,128)(2,1)}) async-done(((bf16[1536,1024]{1,0:T(8,128)(2,1)}, bf16[1536,1024]{1,0:T(8,128)(2,1)}), (bf16[1536,1024]{1,0:T(8,128)(2,1)}, bf16[1536,1024]{1,0:T(8,128)(2,1)})) %all-reduce.3.cloned.1.call-update) | async-done | bytes 6291472 | tf_op jit(solution)/shard_map/psum | solution.py:101
  514.9 0.0 copy-done.5
  514.9 6.7 %convolution_convert_fusion.2 = bf16[1536,768]{1,0:T(8,128)(2,1)S(1)} fusion(bf16[1024,768]{1,0:T(8,128)(2,1)S(1)} %copy-done.5, bf16[1536,1024]{1,0:T(8,128)(2,1)} %get-tuple-element.33, bf16[1536,1024]{1,0:T(8,128)(2,1)} %get-tuple-element.34), kind=kOutput, calls=%fused_computation.20 | convolution fusion | flops 2429681664 | bytes 10223616 | tf_op jit(solution)/shard_map/dot_general | solution.py:103
  521.6 0.0 copy-start.3
  521.6 82.3 %all_to_all.11 = bf16[64,24,768]{2,1,0:T(8,128)(2,1)S(1)} all-to-all(bf16[64,24,768]{2,1,0:T(8,128)(2,1)S(1)} %bitcast.45), channel_id=1, replica_groups=mesh['ctx'=64,'exp'=8] {'ctx'}, dimensions={0} | all-to-all | bytes 4718592 | tf_op jit(solution)/shard_map/all_to_all | solution.py:106
  603.9 0.3 convert_reduce_fusion
  604.2 0.0 copy-done.3
  604.2 0.9 fusion.15
  (8 shorter events, 0.1 us)
Async XLA Ops:
  6.5 345.9 %copy-start = (bf16[1024,768]{1,0:T(8,128)(2,1)S(1)}, bf16[1024,768]{1,0:T(8,128)(2,1)}, u32[]{:S(2)}) copy-start(bf16[1024,768]{1,0:T(8,128)(2,1)} %param.20) | copy-start | bytes 4718596
  6.5 133.1 %all-gather.3.cloned.1.call-start = ((), (), s32[]{:S(2)}) async-start(), calls=%async_computation.2 | async-start | bytes 1064960 | tf_op jit(solution)/shard_map/all_gather | solution.py:32
  7.3 257.9 %all-gather.5.cloned.1.call-start = ((), (), s32[]{:S(2)}) async-start(), calls=%async_computation.3 | async-start | bytes 1064960 | tf_op jit(solution)/shard_map/all_gather | solution.py:33
  8.0 506.9 %all-reduce.3.cloned.1.call-start = ((), (), s32[]{:S(2)}) async-start(), calls=%async_computation.4 | async-start | bytes 12582912 | tf_op jit(solution)/shard_map/psum | solution.py:101
  265.2 6.5 %copy-start.1 = (bf16[64,768]{1,0:T(8,128)(2,1)S(1)}, bf16[64,768]{1,0:T(8,128)(2,1)}, u32[]{:S(2)}) copy-start(bf16[64,768]{1,0:T(8,128)(2,1)} %param.15) | copy-start | bytes 294916
  265.2 17.0 %copy-start.2 = (f32[768]{0:T(1024)S(1)}, f32[768]{0:T(1024)}, u32[]{:S(2)}) copy-start(f32[768]{0:T(1024)} %param.16) | copy-start | bytes 9220
  265.3 2.7 copy-start.6
  352.5 4.2 copy-start.4
  360.8 154.0 %copy-start.5 = (bf16[1024,768]{1,0:T(8,128)(2,1)S(1)}, bf16[1024,768]{1,0:T(8,128)(2,1)}, u32[]{:S(2)}) copy-start(bf16[1024,768]{1,0:T(8,128)(2,1)} %param.21) | copy-start | bytes 4718596
  521.6 82.6 %copy-start.3 = (f32[64]{0:T(128)S(1)}, f32[64]{0:T(128)}, u32[]{:S(2)}) copy-start(f32[64]{0:T(128)} %param.18) | copy-start | bytes 772
Sparse Core Ops, SparseCore 0:
  11.7 127.8 all-gather.2
  144.0 121.1 all-gather.4
  361.0 153.8 all-reduce.2
where the time goes:
time: 612 us
  waiting for transfers between devices  409 us (67%)
  blocking collectives  162 us (26%)
  matrix products  20.8 us (3%)
  between operations  13.2 us (2%)
    psum x1, waiting for transfers between devices, body(): up_full = lax.psum(up_part.astype(jnp.bfloat16), 'exp').astype(jnp.float32)  154 us
    all_gather x1, waiting for transfers between devices, body(): key_shard = lax.all_gather(keys, 'ctx', axis=0, tiled=True)  128 us
    all_gather x1, waiting for transfers between devices, body(): value_shard = lax.all_gather(values, 'ctx', axis=0, tiled=True)  126 us
    all_to_all x1, blocking collectives, body(): lax.all_to_all(down_part.astype(jnp.bfloat16), 'ctx', split_axis=0, conca...  82.3 us
    all_to_all x1, blocking collectives, body(): lax.all_to_all(outgoing, 'ctx', split_axis=0, concat_axis=0, tiled=True)  69.9 us
  transfers between devices with their start and end apart: 3, of which 3 were waited for; matrix products, arithmetic and copies ran while one was open for 1% of the time, Pallas kernels for 0%

commit v1 on v0

--- a/solution.py
+++ b/solution.py
@@ -98,7 +98,9 @@
     gate_part = jnp.einsum("rd,fd->rf", flat_rows, w_gate, preferred_element_type=jnp.float32)
     up_part = jnp.einsum("rd,fd->rf", flat_rows, w_up, preferred_element_type=jnp.float32)
     gate_full = lax.psum(gate_part.astype(jnp.bfloat16), "exp").astype(jnp.float32)
-    up_full = lax.psum(up_part.astype(jnp.bfloat16), "exp").astype(jnp.float32)
+    up_full = jnp.sum(lax.all_gather(up_part.astype(jnp.bfloat16), "exp"), axis=0).astype(
+        jnp.float32
+    )
     hidden = (jax.nn.silu(gate_full) * up_full).astype(jnp.bfloat16)
     down_part = jnp.dot(hidden, w_down, preferred_element_type=jnp.float32).reshape(
         ctx_count, slot_count, feat_local

time: 612 us -> 802 us (1.31)
  the two profiles are of different devices: /device:TPU:40 before, /device:TPU:8 now
where the time goes in v1:
time: 802 us
  waiting for transfers between devices  582 us (73%)
  blocking collectives  160 us (20%)
  matrix products  22.3 us (3%)
  other arithmetic  20.2 us (3%)
  between operations  13.2 us (2%)
    all_gather x1, waiting for transfers between devices, body(): lax.all_gather(up_part.astype(jnp.bfloat16), 'exp')  240 us
    all_gather x1, waiting for transfers between devices, body(): key_shard = lax.all_gather(keys, 'ctx', axis=0, tiled=True)  132 us
    all_gather x1, waiting for transfers between devices, body(): value_shard = lax.all_gather(values, 'ctx', axis=0, tiled=True)  126 us
    psum x1, waiting for transfers between devices, body(): lax.psum(gate_part.astype(jnp.bfloat16), 'exp').astype(jnp.float32)  83 us
    all_to_all x1, blocking collectives, body(): lax.all_to_all(down_part.astype(jnp.bfloat16), 'ctx', split_axis=0, conca...  79.2 us
    all_to_all x1, blocking collectives, body(): lax.all_to_all(outgoing, 'ctx', split_axis=0, concat_axis=0, tiled=True)  70 us
  transfers between devices with their start and end apart: 4, of which 4 were waited for; matrix products, arithmetic and copies ran while one was open for 3% of the time, Pallas kernels for 0%

profile of v1, /device:TPU:8, one launch (start us, length us, event | category | flops | bytes accessed | tf_op | source)
XLA Modules:
  0.0 801.9 jit_solution(9677162956938436703)
XLA Ops:
  6.5 0.0 copy-start
  6.5 0.0 all-gather.5.cloned.1.call-start
  6.5 0.7 all-gather.5.cloned.1.call-update
  7.3 0.0 all-gather.7.cloned.1.call-start
  7.3 0.7 all-gather.7.cloned.1.call-update
  8.0 0.0 all-gather.9.cloned.1.call-start
  8.1 0.7 fusion.22
  8.8 0.1 reduce_window_sum.11
  8.9 1.0 reshape.116
  9.9 0.8 select_reduce_fusion
  10.8 0.7 iota_compare_fusion.3
  11.4 131.6 %all-gather.5.cloned.1.call-done = bf16[4096,128]{1,0:T(8,128)(2,1)} async-done(((bf16[64,128]{1,0:T(8,128)(2,1)}), bf16[4096,128]{1,0:T(8,128)(2,1)}) %all-gather.5.cloned.1.call-update) | async-done | bytes 1048592 | tf_op jit(solution)/shard_map/all_gather | solution.py:32
  143.0 125.6 %all-gather.7.cloned.1.call-done = bf16[4096,128]{1,0:T(8,128)(2,1)} async-done(((bf16[64,128]{1,0:T(8,128)(2,1)}), bf16[4096,128]{1,0:T(8,128)(2,1)}) %all-gather.7.cloned.1.call-update) | async-done | bytes 1048592 | tf_op jit(solution)/shard_map/all_gather | solution.py:33
  268.6 0.0 copy-start.2
  268.6 6.3 conditional.1
  268.6 0.1 add.28
  268.7 0.0 copy-start.7
  268.7 2.6 fusion.29
  271.3 0.0 copy-done.7
  271.4 1.9 fusion.4
  273.3 1.6 fusion.1
  274.9 0.1 divide_convert_fusion
  275.0 0.1 copy.13
  275.1 0.0 copy-done.2
  275.1 0.1 multiply_reduce_fusion
  275.2 10.8 %psum.14 = f32[64]{0:T(128)S(1)} all-reduce(f32[64]{0:T(128)S(1)} %multiply_reduce_fusion), channel_id=1, replica_groups=mesh['ctx'=64,'exp'=8] {'exp'}, use_global_device_ids=true, to_apply=%region_7.8 | all-reduce | flops 64 | bytes 512 | tf_op jit(solution)/shard_map/psum | solution.py:73
  286.1 0.0 copy-done.3
  286.1 0.2 convolution_convert_fusion.3
  286.3 0.2 broadcast_in_dim.22
  286.5 70.0 %all_to_all.10 = bf16[64,24,768]{2,1,0:T(8,128)(2,1)S(1)} all-to-all(bf16[64,24,768]{2,1,0:T(8,128)(2,1)S(1)} %bitcast.44), channel_id=1, replica_groups=mesh['ctx'=64,'exp'=8] {'ctx'}, dimensions={0} | all-to-all | bytes 4718592 | tf_op jit(solution)/shard_map/all_to_all | solution.py:95
  356.4 1.5 copy-done.1
  358.0 0.0 copy-done
  358.0 4.1 convolution_convert_fusion
  362.1 0.0 all-gather.9.cloned.1.call-update
  362.1 0.2 all-reduce.2.cloned.1.call-start
  362.3 1.2 copy-done.5
  363.5 5.7 convolution_convert_fusion.1
  369.2 0.0 all-reduce.2.cloned.1.call-update
  369.2 240.2 %all-gather.9.cloned.1.call-done = bf16[12288,1024]{1,0:T(8,128)(2,1)} async-done(((bf16[1536,1024]{1,0:T(8,128)(2,1)}), bf16[12288,1024]{1,0:T(8,128)(2,1)}) %all-gather.9.cloned.1.call-update) | async-done | bytes 25165840 | tf_op jit(solution)/shard_map/all_gather | solution.py:101
  609.5 15.7 %reduce_sum.52 = bf16[1536,1024]{1,0:T(8,128)(2,1)} reduce(bf16[8,1536,1024]{2,1,0:T(8,128)(2,1)} %bitcast.43, bf16[]{:T(256)} %constant.44.clone.1), dimensions={0}, to_apply=%region_9.10 | reduce | flops 11010048 | bytes 28311554 | tf_op jit(solution)/shard_map/reduce_sum | solution.py:101
  625.1 83.0 %all-reduce.2.cloned.1.call-done = bf16[1536,1024]{1,0:T(8,128)(2,1)} async-done(((bf16[1536,1024]{1,0:T(8,128)(2,1)}), bf16[1536,1024]{1,0:T(8,128)(2,1)}) %all-reduce.2.cloned.1.call-update) | async-done | bytes 3145744 | tf_op jit(solution)/shard_map/psum | solution.py:100
  708.1 0.0 copy-done.6
  708.1 6.7 convolution_convert_fusion.2
  714.8 0.0 copy-start.4
  714.9 79.2 %all_to_all.11 = bf16[64,24,768]{2,1,0:T(8,128)(2,1)S(1)} all-to-all(bf16[64,24,768]{2,1,0:T(8,128)(2,1)S(1)} %bitcast.47), channel_id=1, replica_groups=mesh['ctx'=64,'exp'=8] {'ctx'}, dimensions={0} | all-to-all | bytes 4718592 | tf_op jit(solution)/shard_map/all_to_all | solution.py:108
  794.1 0.3 convert_reduce_fusion
  794.4 0.0 copy-done.4
  794.4 0.9 fusion.15
  (12 shorter events, 0.1 us)
Async XLA Ops:
  6.5 351.4 %copy-start = (bf16[1024,768]{1,0:T(8,128)(2,1)S(1)}, bf16[1024,768]{1,0:T(8,128)(2,1)}, u32[]{:S(2)}) copy-start(bf16[1024,768]{1,0:T(8,128)(2,1)} %param.20) | copy-start | bytes 4718596
  6.5 136.5 %all-gather.5.cloned.1.call-start = ((), (), s32[]{:S(2)}) async-start(), calls=%async_computation.2 | async-start | bytes 1064960 | tf_op jit(solution)/shard_map/all_gather | solution.py:32
  7.3 261.3 %all-gather.7.cloned.1.call-start = ((), (), s32[]{:S(2)}) async-start(), calls=%async_computation.3 | async-start | bytes 1064960 | tf_op jit(solution)/shard_map/all_gather | solution.py:33
  8.0 601.5 %all-gather.9.cloned.1.call-start = ((), (), s32[]{:S(2)}) async-start(), calls=%async_computation.5 | async-start | bytes 28311552 | tf_op jit(solution)/shard_map/all_gather | solution.py:101
  268.6 6.5 copy-start.2
  268.6 17.5 %copy-start.3 = (f32[768]{0:T(1024)S(1)}, f32[768]{0:T(1024)}, u32[]{:S(2)}) copy-start(f32[768]{0:T(1024)} %param.16) | copy-start | bytes 9220
  268.7 2.7 copy-start.7
  356.4 1.5 copy-start.1
  362.1 1.4 copy-start.5
  362.1 346.0 %all-reduce.2.cloned.1.call-start = ((), (), s32[]{:S(2)}) async-start(), calls=%async_computation.4 | async-start | bytes 6291456 | tf_op jit(solution)/shard_map/psum | solution.py:100
  609.5 98.7 %copy-start.6 = (bf16[1024,768]{1,0:T(8,128)(2,1)S(1)}, bf16[1024,768]{1,0:T(8,128)(2,1)}, u32[]{:S(2)}) copy-start(bf16[1024,768]{1,0:T(8,128)(2,1)} %param.21) | copy-start | bytes 4718596
  714.8 79.5 %copy-start.4 = (f32[64]{0:T(128)S(1)}, f32[64]{0:T(128)}, u32[]{:S(2)}) copy-start(f32[64]{0:T(128)} %param.18) | copy-start | bytes 772
Sparse Core Ops, SparseCore 0:
  11.7 131.2 all-gather.4
  147.4 121.1 all-gather.6
  362.2 247.2 all-gather.8
  612.3 95.8 all-reduce.1
